TPU v7x, 32 devices: a whole 2x2x4 slice. The times are simulated.
32 devices in a mesh: groups: 2 (over y), var: 4 (over z), probe: 2 (over x), rep: 2 (over core).
Axes of the slice: x: 2, y: 2, z: 4, core: 2. Of those that a mesh axis runs over, the one named last changes fastest.
Arguments:
- block_values: bfloat16 [512, 6, 128, 128], P(('groups', 'var'), 'rep'), parts along dimension 0, may hold values from -6 to 6
- columns: int32 [512, 6], P(('groups', 'var'), 'rep'), parts along dimension 0, may hold values from 0 to 255, as said below
- probe_signs: int32 [512, 24, 128], P('groups', 'probe'), parts along dimension 0, may hold values from -1 to 1, as said below
Outputs:
- gradient: bfloat16 [512, 6, 128, 128], P(('groups', 'var'), 'rep'), parts along dimension 0
There are 2 independent parts, one for each index of `groups`. A program takes and returns all parts, laid end to end along the dimension named above; each array names one. Nothing has to cross between parts.
Inputs may be any that keep to these rules, and one draw needn't show every extreme that they name: The 6 block columns of each block row are distinct. `probe_signs`: every entry is -1 or 1.
All inputs are finite; a program needn't handle non-finite values.
Results may differ from a plain program's by a relative error of at most 0.015.
Values may be sent and summed in bfloat16 or wider, within the bound.
No kernel may reach another device: no remote copies, remote signals or barrier semaphores. Data moves between devices by JAX's collectives and lax.ppermute only.
A program may use at most 128 MiB of HBM per device.

v0:
```python
import math
import jax
import jax.numpy as jnp
from jax import lax
from jax.sharding import PartitionSpec as P

BLK = 128
KS = 6


def local(block_values, columns, probe_signs):
    rows_here = block_values.shape[0]
    slots_here = block_values.shape[1]
    block_width = block_values.shape[3]
    blocks_all = probe_signs.shape[0]
    probes_here = probe_signs.shape[1]
    inverse = 1.0 / math.sqrt(KS * BLK)
    column_list = columns.reshape(-1)
    total_probes = probes_here * lax.axis_size("probe")
    signs_all = probe_signs.astype(jnp.bfloat16)
    own_rows = lax.dynamic_slice_in_dim(signs_all, lax.axis_index("var") * rows_here, rows_here, 0)

    def select_local(panel_all):
        return jnp.take(panel_all, column_list, axis=0)

    forward_blocks = [select_local(signs_all)]
    back_panels = [own_rows]
    forward_own = own_rows
    for step_index in range(3):
        shaped = forward_blocks[step_index].reshape(rows_here, slots_here, probes_here, block_width)
        product = jnp.einsum(
            "rkij,rksj->rsi", block_values, shaped, preferred_element_type=jnp.float32
        )
        product = lax.psum(product.astype(jnp.bfloat16), "rep").astype(jnp.float32)
        forward_own = (forward_own.astype(jnp.float32) + inverse * product).astype(jnp.bfloat16)
        forward_blocks.append(select_local(lax.all_gather(forward_own, "var", axis=0, tiled=True)))
    for step_index in range(3):
        panel_own = back_panels[step_index]
        weighted = jnp.einsum(
            "rkij,rsi->rksj", block_values, panel_own, preferred_element_type=jnp.float32
        )
        weighted = weighted.reshape(-1, probes_here, block_width)
        contrib = jax.ops.segment_sum(weighted, column_list, num_segments=blocks_all)
        share_rows = blocks_all // (lax.axis_size("var") * lax.axis_size("rep"))
        summed = lax.psum_scatter(
            contrib.astype(jnp.bfloat16), ("var", "rep"), scatter_dimension=0, tiled=True
        ).astype(jnp.float32)
        previous = lax.dynamic_slice_in_dim(
            panel_own, lax.axis_index("rep") * share_rows, share_rows, 0
        )
        updated = (previous.astype(jnp.float32) + inverse * summed).astype(jnp.bfloat16)
        back_panels.append(lax.all_gather(updated, "rep", axis=0, tiled=True))
    left_panels = jnp.stack(back_panels)
    right_blocks = jnp.stack(forward_blocks[::-1]).reshape(
        4, rows_here, slots_here, probes_here, block_width
    )
    estimate = jnp.einsum(
        "trsi,trksj->rkij", left_panels, right_blocks, preferred_element_type=jnp.float32
    )
    estimate = lax.psum(estimate.astype(jnp.bfloat16), "probe").astype(jnp.float32)
    return (estimate / total_probes).astype(jnp.bfloat16)


def solution(mesh):
    return jax.shard_map(
        local,
        mesh=mesh,
        in_specs=(
            P(("groups", "var"), "rep", None, None),
            P(("groups", "var"), "rep"),
            P("groups", "probe", None),
        ),
        out_specs=P(("groups", "var"), "rep", None, None),
        check_vma=False,
    )
```

profile of v0, /device:TPU:0, one launch (start us, length us, event | category | flops | bytes accessed | tf_op | source)
XLA Modules:
  0.0 377.1 jit_solution(8192982231538396565)
XLA Ops:
  8.3 1.6 convert_element_type.87
  11.5 5.4 %convolution_bitcast_fusion.2 = bf16[64,12,128]{2,1,0:T(8,128)(2,1)S(1)} fusion(bf16[64,3,12,128]{3,2,1,0:T(8,128)(2,1)S(1)} %bitcast.66, bf16[64,3,128,128]{3,2,1,0:T(8,128)(2,1)} %param.5), kind=kOutput, calls=%fused_computation.22 | convolution fusion | flops 75497472 | bytes 7077888 | tf_op jit(solution)/shard_map/rkij,rksj->rsi/dot_general | solution.py:31
  18.4 5.1 %fusion.18 = f32[64,12,3,128]{3,1,2,0:T(8,128)} fusion(bf16[64,3,128,128]{3,2,1,0:T(8,128)(2,1)} %param.5, bf16[64,12,128,1]{2,0,1,3:T(8,128)(2,1)S(1)} %get-tuple-element.7), kind=kOutput, calls=%fused_computation.44 | convolution fusion | flops 75497472 | bytes 7667712 | tf_op jit(solution)/shard_map/rkij,rsi->rksj/dot_general | solution.py:39
  23.7 15.5 %scatter_fusion = f32[256,12,128]{2,1,0:T(8,128)S(1)} fusion(f32[256,12,128]{2,1,0:T(8,128)S(1)} %broadcast.14.clone.1, s32[192]{0:T(256)S(1)} %reshape.35, f32[192,12,128]{2,1,0:T(8,128)} %bitcast.64), kind=kCustom, calls=%fused_computation.4 | custom fusion | flops 294912 | bytes 3539712 | tf_op jit(solution)/shard_map/scatter-add | solution.py:43
  39.2 1.4 copy.160
  40.7 1.0 add_convert_fusion.2
  41.7 24.9 %all_gather.18 = bf16[256,12,128]{2,0,1:T(8,128)(2,1)S(1)} all-gather(bf16[64,12,128]{2,0,1:T(8,128)(2,1)S(1)} %add_convert_fusion.2), channel_id=1, replica_groups=mesh['groups'=2,'var'=4,'probe'=2,'rep'=2] {'var'}, dimensions={0}, use_global_device_ids=true | all-gather | bytes 983040 | tf_op jit(solution)/shard_map/all_gather | solution.py:36
  68.2 5.4 %convolution_bitcast_fusion.1 = bf16[64,12,128]{2,1,0:T(8,128)(2,1)S(1)} fusion(bf16[64,3,12,128]{3,2,1,0:T(8,128)(2,1)S(1)} %bitcast.68, bf16[64,3,128,128]{3,2,1,0:T(8,128)(2,1)} %param.5), kind=kOutput, calls=%fused_computation.21 | convolution fusion | flops 75497472 | bytes 7077888 | tf_op jit(solution)/shard_map/rkij,rksj->rsi/dot_general | solution.py:31
  74.5 2.3 reduce-scatter.4.cloned.1.call-done
  77.7 1.9 all_gather.21
  79.6 5.3 %fusion.16 = f32[64,12,3,128]{3,1,2,0:T(8,128)} fusion(bf16[64,3,128,128]{3,2,1,0:T(8,128)(2,1)} %param.5, bf16[64,12,128,1]{2,0,1,3:T(8,128)(2,1)S(1)} %bitcast.72), kind=kOutput, calls=%fused_computation.42 | convolution fusion | flops 75497472 | bytes 7667712 | tf_op jit(solution)/shard_map/rkij,rsi->rksj/dot_general | solution.py:39
  85.1 15.5 %scatter_fusion.1 = f32[256,12,128]{2,1,0:T(8,128)S(1)} fusion(f32[256,12,128]{2,1,0:T(8,128)S(1)} %broadcast.14.clone, s32[192]{0:T(256)S(1)} %reshape.35, f32[192,12,128]{2,1,0:T(8,128)} %bitcast.65), kind=kCustom, calls=%fused_computation.5 | custom fusion | flops 294912 | bytes 3539712 | tf_op jit(solution)/shard_map/scatter-add | solution.py:43
  100.5 1.4 copy.159
  102.0 1.0 add_convert_fusion.1
  103.0 23.0 %all_gather.19 = bf16[256,12,128]{2,0,1:T(8,128)(2,1)S(1)} all-gather(bf16[64,12,128]{2,0,1:T(8,128)(2,1)S(1)} %add_convert_fusion.1), channel_id=1, replica_groups=mesh['groups'=2,'var'=4,'probe'=2,'rep'=2] {'var'}, dimensions={0}, use_global_device_ids=true | all-gather | bytes 983040 | tf_op jit(solution)/shard_map/all_gather | solution.py:36
  127.7 5.1 %convolution_bitcast_fusion = bf16[64,12,128]{2,1,0:T(8,128)(2,1)S(1)} fusion(bf16[64,3,12,128]{3,2,1,0:T(8,128)(2,1)S(1)} %bitcast.70, bf16[64,3,128,128]{3,2,1,0:T(8,128)(2,1)} %param.5), kind=kOutput, calls=%fused_computation.20 | convolution fusion | flops 75497472 | bytes 7077888 | tf_op jit(solution)/shard_map/rkij,rksj->rsi/dot_general | solution.py:31
  134.9 1.9 all_gather.22
  136.8 5.3 %fusion.14 = f32[64,12,3,128]{3,1,2,0:T(8,128)} fusion(bf16[64,3,128,128]{3,2,1,0:T(8,128)(2,1)} %param.5, bf16[64,12,128,1]{2,0,1,3:T(8,128)(2,1)S(1)} %bitcast.73), kind=kOutput, calls=%fused_computation.40 | convolution fusion | flops 75497472 | bytes 7667712 | tf_op jit(solution)/shard_map/rkij,rsi->rksj/dot_general | solution.py:39
  142.3 15.5 %scatter_fusion.2 = f32[256,12,128]{2,1,0:T(8,128)S(1)} fusion(f32[256,12,128]{2,1,0:T(8,128)S(1)} %broadcast.14, s32[192]{0:T(256)S(1)} %reshape.35, f32[192,12,128]{2,1,0:T(8,128)} %bitcast.63), kind=kCustom, calls=%fused_computation.6 | custom fusion | flops 294912 | bytes 3539712 | tf_op jit(solution)/shard_map/scatter-add | solution.py:43
  157.8 1.4 copy.158
  160.1 1.0 add_convert_fusion
  161.1 22.7 %all_gather.20 = bf16[256,12,128]{2,0,1:T(8,128)(2,1)S(1)} all-gather(bf16[64,12,128]{2,0,1:T(8,128)(2,1)S(1)} %add_convert_fusion), channel_id=1, replica_groups=mesh['groups'=2,'var'=4,'probe'=2,'rep'=2] {'var'}, dimensions={0}, use_global_device_ids=true | all-gather | bytes 983040 | tf_op jit(solution)/shard_map/all_gather | solution.py:36
  184.4 1.6 gather_fusion.3
  186.0 1.4 broadcast_select_fusion.3
  187.4 1.8 copy.166
  189.2 1.8 copy.165
  191.7 1.0 add_convert_fusion.3
  192.7 1.9 all_gather.23
  194.8 6.1 %fusion = bf16[64,3,128,128]{2,3,1,0:T(8,128)(2,1)} fusion(bf16[1,64,3,12,128]{4,3,0,2,1:T(8,128)(2,1)S(1)} %bitcast.67, bf16[1,64,3,12,128]{4,3,0,2,1:T(8,128)(2,1)S(1)} %bitcast.69, bf16[1,64,3,12,128]{4,3,0,2,1:T(8,128)(2,1)S(1)} %bitcast.71, bf16[1,64,3,12,128]{4,3,0,2,1:T(8,128)(2,1)S(1)} %bitcast.74, bf16[1,64,12,128]{3,2,0,1:T(8,128)(2,1)S(1)} %bitcast.77, ...), kind=kOutput, calls=%fused_computation.9 | convolution fusion | flops 309854208 | bytes 9437184 | tf_op jit(solution)/shard_map/trsi,trksj->rkij/dot_general | solution.py:57
  200.9 152.0 %all-reduce.11.cloned.1.call-done = bf16[64,3,128,128]{2,3,1,0:T(8,128)(2,1)} async-done(((bf16[64,3,128,128]{2,3,1,0:T(8,128)(2,1)}), bf16[64,3,128,128]{2,3,1,0:T(8,128)(2,1)}) %all-reduce.11.cloned.1.call-update) | async-done | bytes 6291472 | tf_op jit(solution)/shard_map/psum | solution.py:60
  352.9 8.3 %multiply_convert_fusion = bf16[64,3,128,128]{2,3,1,0:T(8,128)(2,1)} fusion(bf16[64,3,128,128]{2,3,1,0:T(8,128)(2,1)} %all-reduce.11.cloned.1.call-done), kind=kLoop, calls=%fused_computation.8 | loop fusion | flops 9437184 | bytes 12582912 | tf_op jit(solution)/shard_map/convert_element_type | solution.py:61
  361.2 8.6 %copy.120 = bf16[64,3,128,128]{3,2,1,0:T(8,128)(2,1)} copy(bf16[64,3,128,128]{2,3,1,0:T(8,128)(2,1)} %multiply_convert_fusion) | data formatting | bytes 12582912 | tf_op jit(solution)/shard_map/convert_element_type | solution.py:61
  (59 shorter events, 14.0 us)
Async XLA Ops:
  7.4 33.3 %all-reduce.5.cloned.1.call-start = ((), (), s32[]{:S(2)}) async-start(), calls=%async_computation.3 | async-start | bytes 393216 | tf_op jit(solution)/shard_map/psum | solution.py:34
  11.5 5.4 %copy-start = (bf16[192,12,128]{2,1,0:T(8,128)(2,1)}, bf16[192,12,128]{2,1,0:T(8,128)(2,1)S(1)}, u32[]{:S(2)}) copy-start(bf16[192,12,128]{2,1,0:T(8,128)(2,1)S(1)} %broadcast_select_fusion.2) | copy-start | bytes 1769476
  17.6 59.1 %reduce-scatter.4.cloned.1.call-start = ((), (), s32[]{:S(2)}) async-start(), calls=%async_computation.6 | async-start | bytes 884736 | tf_op jit(solution)/shard_map/reduce_scatter | solution.py:45
  40.6 61.4 %all-reduce.7.cloned.1.call-start = ((), (), s32[]{:S(2)}) async-start(), calls=%async_computation.4 | async-start | bytes 393216 | tf_op jit(solution)/shard_map/psum | solution.py:34
  68.2 5.4 %copy-start.2 = (bf16[192,12,128]{2,1,0:T(8,128)(2,1)}, bf16[192,12,128]{2,1,0:T(8,128)(2,1)S(1)}, u32[]{:S(2)}) copy-start(bf16[192,12,128]{2,1,0:T(8,128)(2,1)S(1)} %broadcast_select_fusion.1) | copy-start | bytes 1769476
  74.4 59.6 %reduce-scatter.6.cloned.1.call-start = ((), (), s32[]{:S(2)}) async-start(), calls=%async_computation.7 | async-start | bytes 884736 | tf_op jit(solution)/shard_map/reduce_scatter | solution.py:45
  79.6 54.3 %copy-start.4 = (bf16[64,12,128]{2,0,1:T(8,128)(2,1)}, bf16[64,12,128]{2,0,1:T(8,128)(2,1)S(1)}, u32[]{:S(2)}) copy-start(bf16[64,12,128]{2,0,1:T(8,128)(2,1)S(1)} %all_gather.21) | copy-start | bytes 589828
  102.0 58.1 %all-reduce.9.cloned.1.call-start = ((), (), s32[]{:S(2)}) async-start(), calls=%async_computation.5 | async-start | bytes 393216 | tf_op jit(solution)/shard_map/psum | solution.py:34
  133.5 58.2 %reduce-scatter.8.cloned.1.call-start = ((), (), s32[]{:S(2)}) async-start(), calls=%async_computation.8 | async-start | bytes 884736 | tf_op jit(solution)/shard_map/reduce_scatter | solution.py:45
  136.8 5.3 %copy-start.5 = (bf16[64,12,128]{2,0,1:T(8,128)(2,1)}, bf16[64,12,128]{2,0,1:T(8,128)(2,1)S(1)}, u32[]{:S(2)}) copy-start(bf16[64,12,128]{2,0,1:T(8,128)(2,1)S(1)} %all_gather.22) | copy-start | bytes 589828
  142.3 17.0 %copy-start.6 = (bf16[1,64,12,128]{3,1,2,0:T(8,128)(2,1)S(1)}, bf16[1,64,12,128]{3,1,2,0:T(8,128)(2,1)}, u32[]{:S(2)}) copy-start(bf16[1,64,12,128]{3,1,2,0:T(8,128)(2,1)} %get-tuple-element.6) | copy-start | bytes 589828
  159.2 193.7 %all-reduce.11.cloned.1.call-start = ((), (), s32[]{:S(2)}) async-start(), calls=%async_computation.9 | async-start | bytes 12582912 | tf_op jit(solution)/shard_map/psum | solution.py:60
  183.8 11.0 %copy-start.1 = (bf16[192,12,128]{2,1,0:T(8,128)(2,1)S(1)}, bf16[192,12,128]{2,1,0:T(8,128)(2,1)}, u32[]{:S(2)}) copy-start(bf16[192,12,128]{2,1,0:T(8,128)(2,1)} %copy-done) | copy-start | bytes 1769476
  183.8 11.0 %copy-start.3 = (bf16[192,12,128]{2,1,0:T(8,128)(2,1)S(1)}, bf16[192,12,128]{2,1,0:T(8,128)(2,1)}, u32[]{:S(2)}) copy-start(bf16[192,12,128]{2,1,0:T(8,128)(2,1)} %copy-done.2) | copy-start | bytes 1769476
Sparse Core Ops, SparseCore 0:
  17.8 20.7 all-reduce.4
  74.5 18.5 all-reduce.6
  133.6 17.1 all-reduce.8
  201.1 151.8 all-reduce.10
Sparse Core Ops, SparseCore 1:
  40.7 36.0 reduce-scatter.3
  102.0 31.9 reduce-scatter.5
  159.3 32.4 reduce-scatter.7
where the time goes:
time: 379 us; the launch traced here: 377 us
  waiting for transfers between devices  156 us (41%)
  blocking collectives  76.5 us (20%)
  other arithmetic  64.3 us (17%)
  matrix products  37.7 us (10%)
  local copies, waits for them, and re-layouts  27.7 us (7%)
  between operations  15.1 us (4%)
    psum x1, waiting for transfers between devices, local(): lax.psum(estimate.astype(jnp.bfloat16), 'probe').astype(jnp.float32)  152 us
    all_gather x3, blocking collectives, local(): lax.all_gather(forward_own, 'var', axis=0, tiled=True)  70.7 us
    scatter-add x3, other arithmetic, local(): jax.ops.segment_sum(weighted, column_list, num_segments=blocks_all)  46.4 us
    dot_general x3, matrix products, local(): jnp.einsum('rkij,rksj->rsi', block_values, shaped, preferred_element_type...  15.8 us
    dot_general x3, matrix products, local(): jnp.einsum('rkij,rsi->rksj', block_values, panel_own, preferred_element_t...  15.7 us
    convert_element_type x1, local copies, waits for them, and re-layouts, local(): return (estimate / total_probes).astype(jnp.bfloat16)  8.61 us
    convert_element_type x1, other arithmetic, local(): return (estimate / total_probes).astype(jnp.bfloat16)  8.26 us
  transfers between devices with their start and end apart: 7, of which 4 were waited for; matrix products, arithmetic and copies ran while one was open for 25% of the time, Pallas kernels for 0%

commit v1 on v0

--- a/solution.py
+++ b/solution.py
@@ -57,7 +57,13 @@
     estimate = jnp.einsum(
         "trsi,trksj->rkij", left_panels, right_blocks, preferred_element_type=jnp.float32
     )
-    estimate = lax.psum(estimate.astype(jnp.bfloat16), "probe").astype(jnp.float32)
+
+    def vector_fit(local_block, a_name):
+        next_value = jax.lax.all_gather(local_block, a_name)
+        all_values = jnp.sum(next_value, 0)
+        return all_values
+
+    estimate = vector_fit(estimate.astype(jnp.bfloat16), "probe").astype(jnp.float32)
     return (estimate / total_probes).astype(jnp.bfloat16)
 
 

time: 379 us -> 409 us (1.079)
  local copies, waits for them, and re-layouts: 27.7 us -> 45.1 us
  other arithmetic: 64.3 us -> 77.1 us
    psum x1 -> x0, waiting for transfers between devices: 152 us -> none  [local(): lax.psum(estimate.astype(jnp.bfloat16), 'probe').astype(jnp.float32)]
    all_gather x0 -> x1, waiting for transfers between devices: none -> 151 us  [vector_fit(): next_value = jax.lax.all_gather(local_block, a_name)]
    reduce_sum x0 -> x1, other arithmetic: none -> 12.7 us  [vector_fit(): all_values = jnp.sum(next_value, 0)]
    convert_element_type x0 -> x1, local copies, waits for them, and re-layouts: none -> 8.69 us  [local(): estimate.astype(jnp.bfloat16)]
    unnamed x15 -> x16, local copies, waits for them, and re-layouts: 0.8 us -> 9.47 us
  transfers between devices with their start and end apart: 7 -> 7, of which waited for: 4 -> 4; matrix products, arithmetic and copies ran while one was open for 25% -> 23% of each run, Pallas kernels for 0% -> 0%
where the time goes in v1:
time: 409 us; the launch traced here: 407 us
  waiting for transfers between devices  155 us (38%)
  other arithmetic  77.1 us (19%)
  blocking collectives  76.7 us (19%)
  local copies, waits for them, and re-layouts  45.1 us (11%)
  matrix products  37.7 us (9%)
  between operations  15.1 us (4%)
    all_gather x1, waiting for transfers between devices, vector_fit(): next_value = jax.lax.all_gather(local_block, a_name)  151 us
    all_gather x3, blocking collectives, local(): lax.all_gather(forward_own, 'var', axis=0, tiled=True)  70.7 us
    scatter-add x3, other arithmetic, local(): jax.ops.segment_sum(weighted, column_list, num_segments=blocks_all)  46.4 us
    dot_general x3, matrix products, local(): jnp.einsum('rkij,rksj->rsi', block_values, shaped, preferred_element_type...  15.8 us
    dot_general x3, matrix products, local(): jnp.einsum('rkij,rsi->rksj', block_values, panel_own, preferred_element_t...  15.7 us
    reduce_sum x1, other arithmetic, vector_fit(): all_values = jnp.sum(next_value, 0)  12.7 us
    unnamed x16, local copies, waits for them, and re-layouts  9.47 us
    convert_element_type x1, local copies, waits for them, and re-layouts, local(): estimate.astype(jnp.bfloat16)  8.69 us
  transfers between devices with their start and end apart: 7, of which 4 were waited for; matrix products, arithmetic and copies ran while one was open for 23% of the time, Pallas kernels for 0%

profile of v1, /device:TPU:0, one launch (start us, length us, event | category | flops | bytes accessed | tf_op | source)
XLA Modules:
  0.0 406.8 jit_solution(15794500455594584040)
XLA Ops:
  8.3 1.6 convert_element_type.89
  11.5 5.4 %convolution_bitcast_fusion.2 = bf16[64,12,128]{2,1,0:T(8,128)(2,1)S(1)} fusion(bf16[64,3,12,128]{3,2,1,0:T(8,128)(2,1)S(1)} %bitcast.68, bf16[64,3,128,128]{3,2,1,0:T(8,128)(2,1)} %param.5), kind=kOutput, calls=%fused_computation.22 | convolution fusion | flops 75497472 | bytes 7077888 | tf_op jit(solution)/shard_map/rkij,rksj->rsi/dot_general | solution.py:31
  18.4 5.1 %fusion.18 = f32[64,12,3,128]{3,1,2,0:T(8,128)} fusion(bf16[64,3,128,128]{3,2,1,0:T(8,128)(2,1)} %param.5, bf16[64,12,128,1]{2,0,1,3:T(8,128)(2,1)S(1)} %get-tuple-element.7), kind=kOutput, calls=%fused_computation.44 | convolution fusion | flops 75497472 | bytes 7667712 | tf_op jit(solution)/shard_map/rkij,rsi->rksj/dot_general | solution.py:39
  23.7 15.5 %scatter_fusion = f32[256,12,128]{2,1,0:T(8,128)S(1)} fusion(f32[256,12,128]{2,1,0:T(8,128)S(1)} %broadcast.14.clone.1, s32[192]{0:T(256)S(1)} %reshape.35, f32[192,12,128]{2,1,0:T(8,128)} %bitcast.66), kind=kCustom, calls=%fused_computation.4 | custom fusion | flops 294912 | bytes 3539712 | tf_op jit(solution)/shard_map/scatter-add | solution.py:43
  39.2 1.4 copy.167
  40.7 1.0 add_convert_fusion.2
  41.7 24.9 %all_gather.24 = bf16[256,12,128]{2,0,1:T(8,128)(2,1)S(1)} all-gather(bf16[64,12,128]{2,0,1:T(8,128)(2,1)S(1)} %add_convert_fusion.2), channel_id=1, replica_groups=mesh['groups'=2,'var'=4,'probe'=2,'rep'=2] {'var'}, dimensions={0}, use_global_device_ids=true | all-gather | bytes 983040 | tf_op jit(solution)/shard_map/all_gather | solution.py:36
  68.2 5.4 %convolution_bitcast_fusion.1 = bf16[64,12,128]{2,1,0:T(8,128)(2,1)S(1)} fusion(bf16[64,3,12,128]{3,2,1,0:T(8,128)(2,1)S(1)} %bitcast.70, bf16[64,3,128,128]{3,2,1,0:T(8,128)(2,1)} %param.5), kind=kOutput, calls=%fused_computation.21 | convolution fusion | flops 75497472 | bytes 7077888 | tf_op jit(solution)/shard_map/rkij,rksj->rsi/dot_general | solution.py:31
  74.5 2.3 reduce-scatter.4.cloned.1.call-done
  77.7 1.9 all_gather.27
  79.6 5.3 %fusion.16 = f32[64,12,3,128]{3,1,2,0:T(8,128)} fusion(bf16[64,3,128,128]{3,2,1,0:T(8,128)(2,1)} %param.5, bf16[64,12,128,1]{2,0,1,3:T(8,128)(2,1)S(1)} %bitcast.74), kind=kOutput, calls=%fused_computation.42 | convolution fusion | flops 75497472 | bytes 7667712 | tf_op jit(solution)/shard_map/rkij,rsi->rksj/dot_general | solution.py:39
  85.1 15.5 %scatter_fusion.1 = f32[256,12,128]{2,1,0:T(8,128)S(1)} fusion(f32[256,12,128]{2,1,0:T(8,128)S(1)} %broadcast.14.clone, s32[192]{0:T(256)S(1)} %reshape.35, f32[192,12,128]{2,1,0:T(8,128)} %bitcast.67), kind=kCustom, calls=%fused_computation.5 | custom fusion | flops 294912 | bytes 3539712 | tf_op jit(solution)/shard_map/scatter-add | solution.py:43
  100.5 1.4 copy.166
  103.0 23.0 %all_gather.25 = bf16[256,12,128]{2,0,1:T(8,128)(2,1)S(1)} all-gather(bf16[64,12,128]{2,0,1:T(8,128)(2,1)S(1)} %add_convert_fusion.1), channel_id=1, replica_groups=mesh['groups'=2,'var'=4,'probe'=2,'rep'=2] {'var'}, dimensions={0}, use_global_device_ids=true | all-gather | bytes 983040 | tf_op jit(solution)/shard_map/all_gather | solution.py:36
  127.7 5.1 %convolution_bitcast_fusion = bf16[64,12,128]{2,1,0:T(8,128)(2,1)S(1)} fusion(bf16[64,3,12,128]{3,2,1,0:T(8,128)(2,1)S(1)} %bitcast.72, bf16[64,3,128,128]{3,2,1,0:T(8,128)(2,1)} %param.5), kind=kOutput, calls=%fused_computation.20 | convolution fusion | flops 75497472 | bytes 7077888 | tf_op jit(solution)/shard_map/rkij,rksj->rsi/dot_general | solution.py:31
  134.9 1.9 all_gather.28
  136.8 5.3 %fusion.14 = f32[64,12,3,128]{3,1,2,0:T(8,128)} fusion(bf16[64,3,128,128]{3,2,1,0:T(8,128)(2,1)} %param.5, bf16[64,12,128,1]{2,0,1,3:T(8,128)(2,1)S(1)} %bitcast.75), kind=kOutput, calls=%fused_computation.40 | convolution fusion | flops 75497472 | bytes 7667712 | tf_op jit(solution)/shard_map/rkij,rsi->rksj/dot_general | solution.py:39
  142.3 15.5 %scatter_fusion.2 = f32[256,12,128]{2,1,0:T(8,128)S(1)} fusion(f32[256,12,128]{2,1,0:T(8,128)S(1)} %broadcast.14, s32[192]{0:T(256)S(1)} %reshape.35, f32[192,12,128]{2,1,0:T(8,128)} %bitcast.65), kind=kCustom, calls=%fused_computation.6 | custom fusion | flops 294912 | bytes 3539712 | tf_op jit(solution)/shard_map/scatter-add | solution.py:43
  157.8 1.4 copy.165
  161.1 22.7 %all_gather.26 = bf16[256,12,128]{2,0,1:T(8,128)(2,1)S(1)} all-gather(bf16[64,12,128]{2,0,1:T(8,128)(2,1)S(1)} %add_convert_fusion), channel_id=1, replica_groups=mesh['groups'=2,'var'=4,'probe'=2,'rep'=2] {'var'}, dimensions={0}, use_global_device_ids=true | all-gather | bytes 983040 | tf_op jit(solution)/shard_map/all_gather | solution.py:36
  184.4 1.6 gather_fusion.3
  186.0 1.4 broadcast_select_fusion.3
  187.4 1.8 copy.173
  189.2 1.8 copy.172
  192.7 2.2 all_gather.29
  195.0 6.1 %fusion = bf16[64,3,128,128]{2,3,1,0:T(8,128)(2,1)} fusion(bf16[1,64,3,12,128]{4,3,0,2,1:T(8,128)(2,1)S(1)} %bitcast.69, bf16[1,64,3,12,128]{4,3,0,2,1:T(8,128)(2,1)S(1)} %bitcast.71, bf16[1,64,3,12,128]{4,3,0,2,1:T(8,128)(2,1)S(1)} %bitcast.73, bf16[1,64,3,12,128]{4,3,0,2,1:T(8,128)(2,1)S(1)} %bitcast.76, bf16[1,64,12,128]{3,2,0,1:T(8,128)(2,1)S(1)} %bitcast.79, ...), kind=kOutput, calls=%fused_computation.9 | convolution fusion | flops 309854208 | bytes 9437184 | tf_op jit(solution)/shard_map/trsi,trksj->rkij/dot_general | solution.py:57
  201.1 8.7 %copy.124 = bf16[64,3,128,128]{3,2,1,0:T(8,128)(2,1)} copy(bf16[64,3,128,128]{2,3,1,0:T(8,128)(2,1)} %fusion) | data formatting | bytes 12582912 | tf_op jit(solution)/shard_map/convert_element_type | solution.py:66
  209.9 151.3 %all-gather.3.cloned.1.call-done = bf16[128,3,128,128]{3,2,1,0:T(8,128)(2,1)} async-done(((bf16[64,3,128,128]{3,2,1,0:T(8,128)(2,1)}), bf16[128,3,128,128]{3,2,1,0:T(8,128)(2,1)}) %all-gather.3.cloned.1.call-update) | async-done | bytes 12582928 | tf_op jit(solution)/shard_map/all_gather | solution.py:62
  361.2 12.7 %reduce_sum.12 = bf16[64,3,128,128]{3,2,1,0:T(8,128)(2,1)} reduce(bf16[2,64,3,128,128]{4,3,2,1,0:T(8,128)(2,1)} %bitcast.64, bf16[]{:T(256)} %constant.50.clone.1), dimensions={0}, to_apply=%region_9.11 | reduce | flops 3145728 | bytes 18874370 | tf_op jit(solution)/shard_map/reduce_sum | solution.py:63
  373.9 8.7 %copy.149 = bf16[64,3,128,128]{2,3,1,0:T(8,128)(2,1)} copy(bf16[64,3,128,128]{3,2,1,0:T(8,128)(2,1)} %reduce_sum.12) | data formatting | bytes 12582912
  382.6 8.3 %multiply_convert_fusion = bf16[64,3,128,128]{2,3,1,0:T(8,128)(2,1)} fusion(bf16[64,3,128,128]{2,3,1,0:T(8,128)(2,1)} %copy.149), kind=kLoop, calls=%fused_computation.8 | loop fusion | flops 9437184 | bytes 12582912 | tf_op jit(solution)/shard_map/convert_element_type | solution.py:67
  390.8 8.6 %copy.126 = bf16[64,3,128,128]{3,2,1,0:T(8,128)(2,1)} copy(bf16[64,3,128,128]{2,3,1,0:T(8,128)(2,1)} %multiply_convert_fusion) | data formatting | bytes 12582912 | tf_op jit(solution)/shard_map/convert_element_type | solution.py:67
  (62 shorter events, 17.0 us)
Async XLA Ops:
  7.4 33.3 %all-reduce.4.cloned.1.call-start = ((), (), s32[]{:S(2)}) async-start(), calls=%async_computation.3 | async-start | bytes 393216 | tf_op jit(solution)/shard_map/psum | solution.py:34
  11.5 5.4 %copy-start = (bf16[192,12,128]{2,1,0:T(8,128)(2,1)}, bf16[192,12,128]{2,1,0:T(8,128)(2,1)S(1)}, u32[]{:S(2)}) copy-start(bf16[192,12,128]{2,1,0:T(8,128)(2,1)S(1)} %broadcast_select_fusion.2) | copy-start | bytes 1769476
  17.6 59.1 %reduce-scatter.4.cloned.1.call-start = ((), (), s32[]{:S(2)}) async-start(), calls=%async_computation.6 | async-start | bytes 884736 | tf_op jit(solution)/shard_map/reduce_scatter | solution.py:45
  40.6 61.4 %all-reduce.6.cloned.1.call-start = ((), (), s32[]{:S(2)}) async-start(), calls=%async_computation.4 | async-start | bytes 393216 | tf_op jit(solution)/shard_map/psum | solution.py:34
  68.2 5.4 %copy-start.2 = (bf16[192,12,128]{2,1,0:T(8,128)(2,1)}, bf16[192,12,128]{2,1,0:T(8,128)(2,1)S(1)}, u32[]{:S(2)}) copy-start(bf16[192,12,128]{2,1,0:T(8,128)(2,1)S(1)} %broadcast_select_fusion.1) | copy-start | bytes 1769476
  74.4 59.6 %reduce-scatter.6.cloned.1.call-start = ((), (), s32[]{:S(2)}) async-start(), calls=%async_computation.7 | async-start | bytes 884736 | tf_op jit(solution)/shard_map/reduce_scatter | solution.py:45
  79.6 54.3 %copy-start.4 = (bf16[64,12,128]{2,0,1:T(8,128)(2,1)}, bf16[64,12,128]{2,0,1:T(8,128)(2,1)S(1)}, u32[]{:S(2)}) copy-start(bf16[64,12,128]{2,0,1:T(8,128)(2,1)S(1)} %all_gather.27) | copy-start | bytes 589828
  102.0 58.1 %all-reduce.8.cloned.1.call-start = ((), (), s32[]{:S(2)}) async-start(), calls=%async_computation.5 | async-start | bytes 393216 | tf_op jit(solution)/shard_map/psum | solution.py:34
  133.5 58.2 %reduce-scatter.8.cloned.1.call-start = ((), (), s32[]{:S(2)}) async-start(), calls=%async_computation.8 | async-start | bytes 884736 | tf_op jit(solution)/shard_map/reduce_scatter | solution.py:45
  136.8 5.3 %copy-start.5 = (bf16[64,12,128]{2,0,1:T(8,128)(2,1)}, bf16[64,12,128]{2,0,1:T(8,128)(2,1)S(1)}, u32[]{:S(2)}) copy-start(bf16[64,12,128]{2,0,1:T(8,128)(2,1)S(1)} %all_gather.28) | copy-start | bytes 589828
  142.3 17.0 %copy-start.6 = (bf16[1,64,12,128]{3,1,2,0:T(8,128)(2,1)S(1)}, bf16[1,64,12,128]{3,1,2,0:T(8,128)(2,1)}, u32[]{:S(2)}) copy-start(bf16[1,64,12,128]{3,1,2,0:T(8,128)(2,1)} %get-tuple-element.6) | copy-start | bytes 589828
  159.2 202.0 %all-gather.3.cloned.1.call-start = ((), (), s32[]{:S(2)}) async-start(), calls=%async_computation.9 | async-start | bytes 18874368 | tf_op jit(solution)/shard_map/all_gather | solution.py:62
  183.8 11.2 %copy-start.1 = (bf16[192,12,128]{2,1,0:T(8,128)(2,1)S(1)}, bf16[192,12,128]{2,1,0:T(8,128)(2,1)}, u32[]{:S(2)}) copy-start(bf16[192,12,128]{2,1,0:T(8,128)(2,1)} %copy-done) | copy-start | bytes 1769476
  183.8 11.2 %copy-start.3 = (bf16[192,12,128]{2,1,0:T(8,128)(2,1)S(1)}, bf16[192,12,128]{2,1,0:T(8,128)(2,1)}, u32[]{:S(2)}) copy-start(bf16[192,12,128]{2,1,0:T(8,128)(2,1)} %copy-done.2) | copy-start | bytes 1769476
Sparse Core Ops, SparseCore 0:
  17.8 20.7 all-reduce.3
  74.5 18.5 all-reduce.5
  133.6 17.1 all-reduce.7
  210.0 151.1 all-gather.2
Sparse Core Ops, SparseCore 1:
  40.7 36.0 reduce-scatter.3
  102.0 31.9 reduce-scatter.5
  159.3 32.4 reduce-scatter.7
